TPU v7x, 32 devices: a whole 2x2x4 slice. The times are simulated.
32 devices in a mesh: dp: 8 (over z, y), ctx: 4 (over x, core).
Axes of the slice: x: 2, y: 2, z: 4, core: 2. Of those that a mesh axis runs over, the one named last changes fastest.
Arguments:
- tokens: bfloat16 [32768, 768], P(('dp', 'ctx')), may hold values from -6 to 6
- out_grad: bfloat16 [32768, 768], P(('dp', 'ctx')), may hold values from -6 to 6
- positions: int32 [32768], P(('dp', 'ctx')), may hold values from -1 to 2047, as said below
- master: float32 [55392, 128], P(('dp', 'ctx'))
- first_moment: float32 [55392, 128], P(('dp', 'ctx'))
- second_moment: float32 [55392, 128], P(('dp', 'ctx'))
- step_count: int32 [1], replicated, may hold values from 2 to 20
Outputs:
- layer_out: bfloat16 [32768, 768], P(('dp', 'ctx'))
- input_grad: float32 [32768, 768], P(('dp', 'ctx'))
- new_master: float32 [55392, 128], P(('dp', 'ctx'))
- new_first: float32 [55392, 128], P(('dp', 'ctx'))
- new_second: float32 [55392, 128], P(('dp', 'ctx'))
- weight_copy: bfloat16 [55392, 128], P(('dp', 'ctx'))
Inputs may be any that keep to these rules, and one draw needn't show every extreme that they name: `positions`: rows form blocks of 4096, one per index of dp. In a block, sequences of 1024 or 2048 rows start at multiples of 1024 from the block's start, each row holding its place in its sequence (0, 1, 2, ...); a block's first row holds 0, and the rows after its last sequence hold -1.
All inputs are finite; a program needn't handle non-finite values.
Results may differ from a plain program's by a relative error of at most 0.015.
The roundings to bfloat16 on the way count: a program that leaves them out, or rounds other values in their place, can miss the bound.
Values may be sent and summed in bfloat16 or wider, within the bound.
No kernel may reach another device: no remote copies, remote signals or barrier semaphores. Data moves between devices by JAX's collectives and lax.ppermute only.
A program may use at most 448 MiB of HBM per device.

v0:
```python
import jax
import jax.numpy as jnp
from jax import lax
from jax.sharding import PartitionSpec as P

D = 768
HEADS = 12
HEAD_DIM = 64
FF = 3072
SEQ_MIN = 1024
norm_eps = 1e-06


def from_behind(block, axis, distance):
    devices = range(lax.axis_size(axis))
    route = [(i - distance, i) for i in devices if i - distance in devices]
    return lax.ppermute(block, axis, route)


def unpack(flat):
    values = flat.reshape(-1)
    square_size = D * D
    wide_size = D * FF
    in_weight = jnp.concatenate(
        [
            values[0:square_size].reshape(D, D),
            values[square_size : 2 * square_size].reshape(D, D),
            values[2 * square_size : 3 * square_size].reshape(D, D),
        ],
        1,
    )
    out_weight = values[3 * square_size : 4 * square_size].reshape(D, D)
    up_weight = values[4 * square_size : 4 * square_size + wide_size].reshape(D, FF)
    down_weight = values[4 * square_size + wide_size : 4 * square_size + 2 * wide_size].reshape(
        FF, D
    )
    small_start = 4 * square_size + 2 * wide_size
    gain_first = values[small_start : small_start + D].astype(jnp.float32)
    gain_second = values[small_start + D : small_start + 2 * D].astype(jnp.float32)
    conv_taps = (
        values[small_start + 2 * D : small_start + 11 * D].reshape(3, 3 * D).astype(jnp.float32)
    )
    return (in_weight, out_weight, up_weight, down_weight, gain_first, gain_second, conv_taps)


def normalize(values, gain):
    factor = lax.rsqrt(jnp.mean(values * values, axis=-1, keepdims=True) + norm_eps)
    scaled = values * factor
    return (scaled, factor, scaled * gain)


def norm_back(grad_in, scaled, factor, gain):
    weighted = grad_in * gain
    inner_mean = jnp.mean(weighted * scaled, axis=-1, keepdims=True)
    return (factor * (weighted - scaled * inner_mean), jnp.sum(grad_in * scaled, axis=0))


def masked_scores(query_part, key_heads, query_rows, lowest_part, key_index):
    scores = (
        jnp.einsum("qhd,khd->hqk", query_part, key_heads, preferred_element_type=jnp.float32)
        * 0.125
    )
    allowed = (key_index[None, :] <= query_rows[:, None]) & (
        key_index[None, :] >= lowest_part[:, None]
    )
    return jnp.where(allowed[None], scores, -1e30)


def adam_update(master, moment_one, moment_two, gradient, step_count, row_start):
    row_index = row_start + jnp.arange(master.shape[0], dtype=jnp.int32)
    matrix_rows = (4 * D * D + 2 * D * FF) // 128
    out_first = 3 * D * D // 128
    out_last = 4 * D * D // 128
    is_matrix = (row_index < matrix_rows)[:, None]
    is_out = ((row_index >= out_first) & (row_index < out_last))[:, None]
    step_rate = jnp.where(is_matrix, jnp.where(is_out, 0.5, 0.1), 1.0)
    decay_rate = jnp.where(is_matrix, 0.1, 0.0)
    step_value = step_count[0].astype(jnp.float32)
    new_one = 0.9 * moment_one + 0.1 * gradient
    new_two = 0.999 * moment_two + 0.001 * gradient * gradient
    corr_first = 1.0 - jnp.power(0.9, step_value)
    corr_second = 1.0 - jnp.power(0.999, step_value)
    new_weights = master - step_rate * (
        new_one / corr_first / (jnp.sqrt(new_two / corr_second) + 1e-08) + decay_rate * master
    )
    return (new_weights, new_one, new_two)


def shards(tokens, out_grad, positions, master, first_moment, second_moment, step_count):
    rows_here = tokens.shape[0]
    span_rows = min(512, rows_here)
    span_count = rows_here // span_rows
    ctx_count = lax.axis_size("ctx")
    reach_back = min(ctx_count - 1, max(1, 2 * SEQ_MIN // rows_here - 1))
    ctx_place = lax.axis_index("ctx")
    triple_width = 3 * D
    shard_low = master.astype(jnp.bfloat16)
    gathered = lax.all_gather(shard_low, ("dp", "ctx"), axis=0, tiled=True)
    in_weight, out_weight, up_weight, down_weight, gain_first, gain_second, conv_taps = unpack(
        gathered
    )
    inputs = tokens.astype(jnp.float32)
    scaled_one, factor_one, normed_one = normalize(inputs, gain_first)
    normed_low = normed_one.astype(jnp.bfloat16)
    projected = jnp.dot(normed_low, in_weight, preferred_element_type=jnp.float32).astype(
        jnp.bfloat16
    )
    rim_rows = from_behind(projected[rows_here - 2 :], "ctx", 1)
    extended = jnp.concatenate([rim_rows, projected], 0).astype(jnp.float32)
    after_one = (positions >= 1).astype(jnp.float32)[:, None]
    after_two = (positions >= 2).astype(jnp.float32)[:, None]
    mixed_full = (
        conv_taps[0] * extended[2:]
        + after_one * conv_taps[1] * extended[1:-1]
        + after_two * conv_taps[2] * extended[:-2]
    )
    mixed_low = mixed_full.astype(jnp.bfloat16)
    query_heads = mixed_low[:, :D].reshape(rows_here, HEADS, HEAD_DIM)
    own_pairs = mixed_low[:, D:]
    earlier = [from_behind(own_pairs, "ctx", 1)]
    key_values = jnp.concatenate(earlier + [own_pairs], 0)
    key_heads = key_values[:, :D].reshape(-1, HEADS, HEAD_DIM)
    value_heads = key_values[:, D:].reshape(-1, HEADS, HEAD_DIM)
    key_index = (ctx_place - reach_back) * rows_here + jnp.arange(
        key_values.shape[0], dtype=jnp.int32
    )
    query_index = ctx_place * rows_here + jnp.arange(rows_here, dtype=jnp.int32)
    lowest = query_index - jnp.maximum(positions, 0)
    attended = []
    log_totals = []
    for span_at in range(span_count):
        rows_part = slice(span_at * span_rows, (span_at + 1) * span_rows)
        scores = masked_scores(
            query_heads[rows_part], key_heads, query_index[rows_part], lowest[rows_part], key_index
        )
        peak_score = jnp.max(scores, axis=-1, keepdims=True)
        raised = jnp.exp(scores - peak_score)
        total_sum = jnp.sum(raised, axis=-1, keepdims=True)
        probs_low = (raised / total_sum).astype(jnp.bfloat16)
        span_out = jnp.einsum(
            "hqk,khd->qhd", probs_low, value_heads, preferred_element_type=jnp.float32
        )
        attended.append(span_out.reshape(span_rows, D))
        log_totals.append(peak_score + jnp.log(total_sum))
    attn_low = jnp.concatenate(attended, 0).astype(jnp.bfloat16)
    hidden = inputs + jnp.dot(attn_low, out_weight, preferred_element_type=jnp.float32)
    scaled_two, factor_two, normed_two = normalize(hidden, gain_second)
    second_low = normed_two.astype(jnp.bfloat16)
    before = jnp.dot(second_low, up_weight, preferred_element_type=jnp.float32)
    active = jnp.maximum(before, 0.0)
    squared_low = (active * active).astype(jnp.bfloat16)
    layer_out = (
        hidden + jnp.dot(squared_low, down_weight, preferred_element_type=jnp.float32)
    ).astype(jnp.bfloat16)
    regathered = lax.all_gather(shard_low, ("dp", "ctx"), axis=0, tiled=True)
    in_weight, out_weight, up_weight, down_weight, gain_first, gain_second, conv_taps = unpack(
        regathered
    )
    fetched = [from_behind(own_pairs, "ctx", 1)]
    key_values = jnp.concatenate(fetched + [own_pairs], 0)
    key_heads = key_values[:, :D].reshape(-1, HEADS, HEAD_DIM)
    value_heads = key_values[:, D:].reshape(-1, HEADS, HEAD_DIM)
    grad_out = out_grad.astype(jnp.float32) * (positions >= 0).astype(jnp.float32)[:, None]
    grad_low = grad_out.astype(jnp.bfloat16)
    grad_down = jnp.einsum("tf,td->fd", squared_low, grad_low, preferred_element_type=jnp.float32)
    grad_squared = jnp.einsum(
        "td,fd->tf", grad_low, down_weight, preferred_element_type=jnp.float32
    )
    grad_before = (grad_squared * 2.0 * active).astype(jnp.bfloat16)
    grad_up = jnp.einsum("td,tf->df", second_low, grad_before, preferred_element_type=jnp.float32)
    grad_normed_two = jnp.einsum(
        "tf,df->td", grad_before, up_weight, preferred_element_type=jnp.float32
    )
    back_two, grad_gain_two = norm_back(grad_normed_two, scaled_two, factor_two, gain_second)
    grad_hidden = grad_out + back_two
    hidden_low = grad_hidden.astype(jnp.bfloat16)
    grad_outw = jnp.einsum("td,te->de", attn_low, hidden_low, preferred_element_type=jnp.float32)
    grad_attended = jnp.einsum(
        "te,de->td", hidden_low, out_weight, preferred_element_type=jnp.float32
    ).astype(jnp.bfloat16)
    grad_heads = grad_attended.reshape(rows_here, HEADS, HEAD_DIM)
    grad_query_parts = []
    grad_keys = jnp.zeros(key_heads.shape, jnp.float32)
    grad_values = jnp.zeros(value_heads.shape, jnp.float32)
    for span_at in range(span_count):
        rows_part = slice(span_at * span_rows, (span_at + 1) * span_rows)
        scores = masked_scores(
            query_heads[rows_part], key_heads, query_index[rows_part], lowest[rows_part], key_index
        )
        probs_full = jnp.exp(scores - log_totals[span_at])
        probs_low = probs_full.astype(jnp.bfloat16)
        grad_probs = jnp.einsum(
            "qhd,khd->hqk", grad_heads[rows_part], value_heads, preferred_element_type=jnp.float32
        )
        inner_sum = jnp.sum(probs_full * grad_probs, axis=-1, keepdims=True)
        grad_scores = (probs_full * (grad_probs - inner_sum)).astype(jnp.bfloat16)
        grad_query_parts.append(
            jnp.einsum("hqk,khd->qhd", grad_scores, key_heads, preferred_element_type=jnp.float32)
            * 0.125
        )
        grad_keys = (
            grad_keys
            + jnp.einsum(
                "hqk,qhd->khd",
                grad_scores,
                query_heads[rows_part],
                preferred_element_type=jnp.float32,
            )
            * 0.125
        )
        grad_values = grad_values + jnp.einsum(
            "hqk,qhd->khd", probs_low, grad_heads[rows_part], preferred_element_type=jnp.float32
        )
    grad_query = jnp.concatenate(grad_query_parts, 0).reshape(rows_here, D)
    grad_pairs = jnp.concatenate([grad_keys.reshape(-1, D), grad_values.reshape(-1, D)], 1)
    own_grad = grad_pairs[reach_back * rows_here :]
    piece_rows = grad_pairs[(reach_back - 1) * rows_here : (reach_back - 1 + 1) * rows_here]
    own_grad = own_grad + from_behind(piece_rows.astype(jnp.bfloat16), "ctx", -1).astype(
        piece_rows.dtype
    )
    grad_mixed = jnp.concatenate([grad_query, own_grad], 1)
    lead_rows = jnp.stack(
        [
            conv_taps[2] * after_two[0] * grad_mixed[0],
            conv_taps[1] * after_one[0] * grad_mixed[0]
            + conv_taps[2] * after_two[1] * grad_mixed[1],
        ]
    )
    tail_rows = from_behind(lead_rows, "ctx", -1)
    grad_projected = (
        conv_taps[0] * grad_mixed
        + jnp.concatenate(
            [
                conv_taps[1] * after_one[1:] * grad_mixed[1:],
                jnp.zeros((1, triple_width), jnp.float32),
            ],
            0,
        )
        + jnp.concatenate(
            [
                conv_taps[2] * after_two[2:] * grad_mixed[2:],
                jnp.zeros((2, triple_width), jnp.float32),
            ],
            0,
        )
        + jnp.concatenate([jnp.zeros((rows_here - 2, triple_width), jnp.float32), tail_rows], 0)
    )
    tap_grads = jnp.stack(
        [
            jnp.sum(grad_mixed * extended[2:], axis=0),
            jnp.sum(after_one * grad_mixed * extended[1:-1], axis=0),
            jnp.sum(after_two * grad_mixed * extended[:-2], axis=0),
        ]
    )
    projected_grad_low = grad_projected.astype(jnp.bfloat16)
    grad_inw = jnp.einsum(
        "td,te->de", normed_low, projected_grad_low, preferred_element_type=jnp.float32
    )
    grad_normed_one = jnp.einsum(
        "te,de->td", projected_grad_low, in_weight, preferred_element_type=jnp.float32
    )
    back_one, grad_gain_one = norm_back(grad_normed_one, scaled_one, factor_one, gain_first)
    input_grad = grad_hidden + back_one
    total_rows = gathered.shape[0]
    used_count = 4 * D * D + 2 * D * FF + 11 * D
    flat_grad = jnp.concatenate(
        [
            grad_inw[:, :D].reshape(-1),
            grad_inw[:, D : 2 * D].reshape(-1),
            grad_inw[:, 2 * D :].reshape(-1),
            grad_outw.reshape(-1),
            grad_up.reshape(-1),
            grad_down.reshape(-1),
            grad_gain_one,
            grad_gain_two,
            tap_grads.reshape(-1),
            jnp.zeros((total_rows * 128 - used_count,), jnp.float32),
        ]
    ).reshape(total_rows, 128)
    grad_shard = lax.psum_scatter(flat_grad, ("dp", "ctx"), scatter_dimension=0, tiled=True)
    row_start = lax.axis_index(("dp", "ctx")) * master.shape[0]
    new_weights, new_one, new_two = adam_update(
        master, first_moment, second_moment, grad_shard, step_count, row_start
    )
    return (layer_out, input_grad, new_weights, new_one, new_two, new_weights.astype(jnp.bfloat16))


def solution(mesh):
    return jax.shard_map(
        shards,
        mesh=mesh,
        in_specs=(
            P(("dp", "ctx"), None),
            P(("dp", "ctx"), None),
            P(("dp", "ctx")),
            P(("dp", "ctx"), None),
            P(("dp", "ctx"), None),
            P(("dp", "ctx"), None),
            P(),
        ),
        out_specs=(
            P(("dp", "ctx"), None),
            P(("dp", "ctx"), None),
            P(("dp", "ctx"), None),
            P(("dp", "ctx"), None),
            P(("dp", "ctx"), None),
            P(("dp", "ctx"), None),
        ),
        check_vma=False,
    )
```

profile of v0, /device:TPU:1, one launch (start us, length us, event | category | flops | bytes accessed | tf_op | source)
XLA Modules:
  0.0 1157.4 jit_solution(14164347562141519024)
XLA Ops:
  22.5 95.1 %all-gather.3.cloned.1.call-done = bf16[32,1731,128]{2,1,0:T(8,128)(2,1)} async-done(((bf16[1,1731,128]{2,1,0:T(8,128)(2,1)}), bf16[32,1731,128]{2,1,0:T(8,128)(2,1)}) %all-gather.3.cloned.1.call-update) | async-done | bytes 14180368 | tf_op jit(solution)/shard_map/all_gather | solution.py:98
  117.6 11.5 reshape.356
  216.8 21.5 %fusion.13 = (f32[12,512]{1,0:T(8,128)S(1)}, f32[12,512,2048]{2,1,0:T(8,128)}) fusion(pred[512,2048]{1,0:T(8,128)(4,1)} %get-tuple-element.61, bf16[512,12,64]{0,2,1:T(8,128)(2,1)} %bitcast.124, bf16[2048,12,64]{0,2,1:T(8,128)(2,1)S(1)} %bitcast.103), kind=kOutput, calls=%fused_computation.27 | convolution fusion | flops 1648355328 | bytes 55336960 | tf_op jit(solution)/shard_map/qhd,khd->hqk/dot_general | solution.py:60
  238.4 22.9 %fusion.1 = f32[12,512]{1,0:T(8,128)S(1)} fusion(f32[12,512]{1,0:T(8,128)S(1)} %get-tuple-element.74, f32[12,512,2048]{2,1,0:T(8,128)} %get-tuple-element.75, pred[512,2048]{1,0:T(8,128)(4,1)} %get-tuple-element.61), kind=kLoop, calls=%fused_computation.12 | loop fusion | flops 50325504 | bytes 51429376 | tf_op jit(solution)/shard_map/reduce_sum | solution.py:138
  261.9 21.9 %fusion.40 = bf16[12,64,512]{2,1,0:T(8,128)(2,1)} fusion(bf16[2048,12,64]{0,2,1:T(8,128)(2,1)} %bitcast.114, f32[12,512]{1,0:T(8,128)S(1)} %fusion.1, f32[12,512]{1,0:T(8,128)S(1)} %get-tuple-element.74, f32[12,512,2048]{2,1,0:T(8,128)} %get-tuple-element.75, pred[512,2048]{1,0:T(8,128)(4,1)S(1)} %copy-done.4), kind=kOutput, calls=%fused_computation.90 | convolution fusion | flops 1673920512 | bytes 55361536 | tf_op jit(solution)/shard_map/hqk,khd->qhd/dot_general | solution.py:140
  283.8 21.5 %fusion.14 = (f32[12,512]{1,0:T(8,128)S(1)}, f32[12,512,2048]{2,1,0:T(8,128)}) fusion(pred[512,2048]{1,0:T(8,128)(4,1)} %get-tuple-element.62, bf16[512,12,64]{0,2,1:T(8,128)(2,1)} %bitcast.122, bf16[2048,12,64]{0,2,1:T(8,128)(2,1)S(1)} %bitcast.104), kind=kOutput, calls=%fused_computation.28 | convolution fusion | flops 1648355328 | bytes 55336960 | tf_op jit(solution)/shard_map/qhd,khd->hqk/dot_general | solution.py:60
  305.3 22.9 %fusion.2 = f32[12,512]{1,0:T(8,128)S(1)} fusion(f32[12,512]{1,0:T(8,128)S(1)} %get-tuple-element.72, f32[12,512,2048]{2,1,0:T(8,128)} %get-tuple-element.73, pred[512,2048]{1,0:T(8,128)(4,1)} %get-tuple-element.62), kind=kLoop, calls=%fused_computation.13 | loop fusion | flops 50325504 | bytes 51429376 | tf_op jit(solution)/shard_map/reduce_sum | solution.py:138
  328.2 22.0 %fusion.39 = bf16[12,64,512]{2,1,0:T(8,128)(2,1)} fusion(bf16[2048,12,64]{0,2,1:T(8,128)(2,1)} %bitcast.115, f32[12,512]{1,0:T(8,128)S(1)} %fusion.2, f32[12,512]{1,0:T(8,128)S(1)} %get-tuple-element.72, f32[12,512,2048]{2,1,0:T(8,128)} %get-tuple-element.73, pred[512,2048]{1,0:T(8,128)(4,1)S(1)} %copy-done.3), kind=kOutput, calls=%fused_computation.89 | convolution fusion | flops 1673920512 | bytes 55361536 | tf_op jit(solution)/shard_map/hqk,khd->qhd/dot_general | solution.py:140
  362.1 10.5 add_convert_fusion.2
  372.6 10.3 multiply_convert_fusion.2
  382.9 12.6 %fusion.38 = f32[3072,768]{1,0:T(8,128)} fusion(f32[1024,3072]{1,0:T(8,128)} %fusion.73, bf16[1024,768]{0,1:T(8,128)(2,1)S(1)} %copy-done.16, f32[1024]{0:T(1024)S(1)} %copy-done.43), kind=kOutput, calls=%fused_computation.85 | convolution fusion | flops 4843634688 | bytes 23597056 | tf_op jit(solution)/shard_map/tf,td->fd/dot_general | solution.py:165
  415.8 22.9 %fusion.5 = f32[12,64,2048]{2,1,0:T(8,128)} fusion(bf16[512,12,64]{0,2,1:T(8,128)(2,1)S(1)} %bitcast.131, f32[12,512]{1,0:T(8,128)S(1)} %log_add_fusion, f32[12,512,2048]{2,1,0:T(8,128)} %get-tuple-element.73, pred[512,2048]{1,0:T(8,128)(4,1)S(1)} %copy-done.3), kind=kOutput, calls=%fused_computation.16 | convolution fusion | flops 1660944384 | bytes 58482688 | tf_op jit(solution)/shard_map/hqk,qhd->khd/dot_general | solution.py:211
  438.8 37.1 %multiply_reduce_fusion = (f32[12,512]{1,0:T(8,128)S(1)}, f32[12,512,2048]{2,1,0:T(8,128)}) fusion(f32[12,512]{1,0:T(8,128)S(1)} %log_add_fusion, f32[12,512,2048]{2,1,0:T(8,128)} %get-tuple-element.73, pred[512,2048]{1,0:T(8,128)(4,1)S(1)} %copy-done.3, bf16[512,12,64]{0,2,1:T(8,128)(2,1)S(1)} %bitcast.132, bf16[2048,12,64]{0,2,1:T(8,128)(2,1)} %bitcast.116), kind=kOutput, calls=%fused_computation.1 | convolution fusion | flops 1673521152 | bytes 105693184 | tf_op jit(solution)/shard_map/qhd,khd->hqk/dot_general | solution.py:192
  478.5 11.1 reshape.350
  502.3 37.1 %multiply_reduce_fusion.1 = (f32[12,512]{1,0:T(8,128)S(1)}, f32[12,512,2048]{2,1,0:T(8,128)}) fusion(f32[12,512]{1,0:T(8,128)S(1)} %copy-done.21, f32[12,512,2048]{2,1,0:T(8,128)} %get-tuple-element.75, pred[512,2048]{1,0:T(8,128)(4,1)S(1)} %copy-done.5, bf16[512,12,64]{0,2,1:T(8,128)(2,1)S(1)} %bitcast.129, bf16[2048,12,64]{0,2,1:T(8,128)(2,1)} %bitcast.117), kind=kOutput, calls=%fused_computation.4 | convolution fusion | flops 1673521152 | bytes 105693184 | tf_op jit(solution)/shard_map/qhd,khd->hqk/dot_general | solution.py:192
  539.5 25.3 %fusion.26 = f32[12,64,2048]{2,1,0:T(8,128)} fusion(f32[12,64,2048]{2,1,0:T(8,128)} %fusion.5, bf16[512,12,64]{0,2,1:T(8,128)(2,1)S(1)} %bitcast.130, f32[12,512]{1,0:T(8,128)S(1)} %copy-done.21, f32[12,512,2048]{2,1,0:T(8,128)} %get-tuple-element.75, pred[512,2048]{1,0:T(8,128)(4,1)S(1)} %copy-done.5), kind=kOutput, calls=%fused_computation.65 | convolution fusion | flops 1662517248 | bytes 64774144 | tf_op jit(solution)/shard_map/hqk,qhd->khd/dot_general | solution.py:211
  571.4 40.6 %multiply_convert_fusion.1 = bf16[12,512,2048]{2,1,0:T(8,128)(2,1)} fusion(f32[12,512,2048]{2,1,0:T(8,128)} %get-tuple-element.80, f32[12,512]{1,0:T(8,128)S(1)} %get-tuple-element.79, f32[12,512]{1,0:T(8,128)S(1)} %copy-done.21, f32[12,512,2048]{2,1,0:T(8,128)} %get-tuple-element.75, pred[512,2048]{1,0:T(8,128)(4,1)S(1)} %copy-done.5), kind=kLoop, calls=%fused_computation.3 | loop fusion | flops 75497472 | bytes 126926848 | tf_op jit(solution)/shard_map/convert_element_type | solution.py:196
  612.0 15.4 %fusion.85 = f32[12,64,2048]{2,1,0:T(8,128)} fusion(bf16[512,12,64]{0,2,1:T(8,128)(2,1)S(1)} %bitcast.125, bf16[12,512,2048]{2,1,0:T(8,128)(2,1)} %multiply_convert_fusion.1), kind=kOutput, calls=%fused_computation.173 | convolution fusion | flops 1610612736 | bytes 32243712 | tf_op jit(solution)/shard_map/hqk,qhd->khd/dot_general | solution.py:203
  627.4 40.4 %multiply_convert_fusion = bf16[12,512,2048]{2,1,0:T(8,128)(2,1)} fusion(f32[12,512,2048]{2,1,0:T(8,128)} %get-tuple-element.82, f32[12,512]{1,0:T(8,128)S(1)} %get-tuple-element.81, f32[12,512]{1,0:T(8,128)S(1)} %log_add_fusion, f32[12,512,2048]{2,1,0:T(8,128)} %get-tuple-element.73, pred[512,2048]{1,0:T(8,128)(4,1)S(1)} %copy-done.3), kind=kLoop, calls=%fused_computation | loop fusion | flops 75497472 | bytes 126926848 | tf_op jit(solution)/shard_map/convert_element_type | solution.py:196
  667.8 17.2 %add_multiply_fusion = f32[12,64,2048]{2,1,0:T(8,128)} fusion(f32[12,64,2048]{2,1,0:T(8,128)} %fusion.85, bf16[512,12,64]{0,2,1:T(8,128)(2,1)S(1)} %bitcast.123, bf16[12,512,2048]{2,1,0:T(8,128)(2,1)} %multiply_convert_fusion), kind=kOutput, calls=%fused_computation.52 | convolution fusion | flops 1613758464 | bytes 38535168 | tf_op jit(solution)/shard_map/hqk,qhd->khd/dot_general | solution.py:203
  698.5 13.7 %multiply_bitcast_fusion.1 = f32[512,12,64]{0,2,1:T(8,128)} fusion(bf16[2048,12,64]{0,2,1:T(8,128)(2,1)S(1)} %bitcast.105, bf16[12,512,2048]{2,1,0:T(8,128)(2,1)} %multiply_convert_fusion.1), kind=kOutput, calls=%fused_computation.88 | convolution fusion | flops 1611005952 | bytes 29884416 | tf_op jit(solution)/shard_map/hqk,khd->qhd/dot_general | solution.py:198
  712.2 13.7 %multiply_bitcast_fusion = f32[512,12,64]{0,2,1:T(8,128)} fusion(bf16[2048,12,64]{0,2,1:T(8,128)(2,1)S(1)} %bitcast.106, bf16[12,512,2048]{2,1,0:T(8,128)(2,1)} %multiply_convert_fusion), kind=kOutput, calls=%fused_computation.87 | convolution fusion | flops 1611005952 | bytes 29884416 | tf_op jit(solution)/shard_map/hqk,khd->qhd/dot_general | solution.py:198
  753.6 13.7 %multiply_reduce_fusion.4 = (f32[2304]{0:T(1024)S(1)}, f32[2304]{0:T(1024)S(1)}, f32[2304]{0:T(1024)S(1)}, bf16[1024,2304]{1,0:T(8,128)(2,1)}) fusion(f32[1026,2304]{1,0:T(8,128)S(1)} %bitcast.102, f32[1024,1536]{1,0:T(8,128)S(1)} %fusion.20, f32[1024,768]{1,0:T(8,128)S(1)} %copy.63, f32[1024]{0:T(1024)S(1)} %copy-done.31, f32[1024]{0:T(1024)S(1)} %copy-done.33, ...), kind=kLoop, calls=%fused_computation.43 | loop fusion | flops 33023232 | bytes 61377536 | tf_op jit(solution)/shard_map/reduce_sum | solution.py:250
  823.2 307.1 %fusion = f32[1744,128]{1,0:T(8,128)S(1)} fusion(f32[55392,128]{1,0:T(8,128)} %bitcast.26), kind=kCustom, calls=%all-reduce-scatter | all-reduce-scatter fusion | flops 7143425 | bytes 29253632
  (248 shorter events, 273.0 us)
Async XLA Ops:
  7.2 110.4 %all-gather.3.cloned.1.call-start = ((), (), s32[]{:S(2)}) async-start(), calls=%async_computation | async-start | bytes 14665728 | tf_op jit(solution)/shard_map/all_gather | solution.py:98
  10.5 148.5 %copy-start.30 = (f32[1024]{0:T(1024)}, f32[1024]{0:T(1024)S(1)}, u32[]{:S(2)}) copy-start(f32[1024]{0:T(1024)S(1)} %get-tuple-element.66) | copy-start | bytes 12292
  10.5 148.5 %copy-start.32 = (f32[1024]{0:T(1024)}, f32[1024]{0:T(1024)S(1)}, u32[]{:S(2)}) copy-start(f32[1024]{0:T(1024)S(1)} %get-tuple-element.67) | copy-start | bytes 12292
  14.8 133.1 %copy-start.7 = (bf16[1024,768]{0,1:T(8,128)(2,1)}, bf16[1024,768]{0,1:T(8,128)(2,1)S(1)}, u32[]{:S(2)}) copy-start(bf16[1024,768]{0,1:T(8,128)(2,1)S(1)} %copy.53) | copy-start | bytes 4718596
  19.6 128.4 %copy-start.41 = (f32[1024]{0:T(1024)}, f32[1024]{0:T(1024)S(1)}, u32[]{:S(2)}) copy-start(f32[1024]{0:T(1024)S(1)} %add_rsqrt_fusion.1) | copy-start | bytes 12292
  130.4 17.6 %copy-start.39 = (f32[768]{0:T(1024)}, f32[768]{0:T(1024)S(1)}, u32[]{:S(2)}) copy-start(f32[768]{0:T(1024)S(1)} %get-tuple-element.38) | copy-start | bytes 9220
  152.5 5.6 collective-permute-start
  165.8 37.3 %collective-permute-start.1 = (bf16[1024,1536]{1,0:T(8,128)(2,1)}, bf16[1024,1536]{1,0:T(8,128)(2,1)}, u32[]{:S(2)}, u32[]{:S(2)}) collective-permute-start(bf16[1024,1536]{1,0:T(8,128)(2,1)} %slice.244), channel_id=1, source_target_pairs={{0,1},{1,2},{2,3},{4,5},{5,6},{6,7},{8,9},{9,10},{10,11},{12,13},{... | collective-permute-start | bytes 9437192 | tf_op jit(solution)/shard_map/ppermute | solution.py:17
  211.4 72.4 %copy-start.1 = (bf16[2048,768]{0,1:T(8,128)(2,1)}, bf16[2048,768]{0,1:T(8,128)(2,1)S(1)}, u32[]{:S(2)}) copy-start(bf16[2048,768]{0,1:T(8,128)(2,1)S(1)} %copy.56) | copy-start | bytes 9437188
  238.4 23.6 %copy-start.4 = (pred[512,2048]{1,0:T(8,128)(4,1)S(1)}, pred[512,2048]{1,0:T(8,128)(4,1)}, u32[]{:S(2)}) copy-start(pred[512,2048]{1,0:T(8,128)(4,1)} %get-tuple-element.61) | copy-start | bytes 3145732
  305.3 22.9 %copy-start.3 = (pred[512,2048]{1,0:T(8,128)(4,1)S(1)}, pred[512,2048]{1,0:T(8,128)(4,1)}, u32[]{:S(2)}) copy-start(pred[512,2048]{1,0:T(8,128)(4,1)} %get-tuple-element.62) | copy-start | bytes 3145732
  328.2 22.1 %copy-start.8 = (bf16[1024,768]{0,1:T(8,128)(2,1)S(1)}, bf16[1024,768]{0,1:T(8,128)(2,1)}, u32[]{:S(2)}) copy-start(bf16[1024,768]{0,1:T(8,128)(2,1)} %copy-done.7) | copy-start | bytes 4718596
  328.2 22.1 %copy-start.20 = (bf16[768,768]{1,0:T(8,128)(2,1)S(1)}, bf16[768,768]{1,0:T(8,128)(2,1)}, u32[]{:S(2)}) copy-start(bf16[768,768]{1,0:T(8,128)(2,1)} %reshape.339) | copy-start | bytes 3538948
  353.5 19.1 %slice-start.15 = ((s8[4718592]{0:T(1024)(128)(4,1)}), s8[4194304]{0:T(1024)(128)(4,1)S(1)}, s32[]{:S(2)}) async-start(s8[4718592]{0:T(1024)(128)(4,1)} %bitcast.127), calls=%async_computation.16 | async-start | bytes 8388608
  489.6 12.7 %copy-start.5 = (pred[512,2048]{1,0:T(8,128)(4,1)S(1)}, pred[512,2048]{1,0:T(8,128)(4,1)}, u32[]{:S(2)}) copy-start(pred[512,2048]{1,0:T(8,128)(4,1)} %get-tuple-element.61) | copy-start | bytes 3145732
  571.4 40.6 %copy-start.15 = (bf16[512,768]{0,1:T(8,128)(2,1)S(1)}, bf16[512,768]{0,1:T(8,128)(2,1)}, u32[]{:S(2)}) copy-start(bf16[512,768]{0,1:T(8,128)(2,1)} %copy.55) | copy-start | bytes 2359300
  627.4 40.4 %copy-start.14 = (bf16[512,768]{0,1:T(8,128)(2,1)S(1)}, bf16[512,768]{0,1:T(8,128)(2,1)}, u32[]{:S(2)}) copy-start(bf16[512,768]{0,1:T(8,128)(2,1)} %copy.57) | copy-start | bytes 2359300
  696.6 39.6 %collective-permute-start.2 = (bf16[1024,1536]{1,0:T(8,128)(2,1)}, bf16[1024,1536]{1,0:T(8,128)(2,1)}, u32[]{:S(2)}, u32[]{:S(2)}) collective-permute-start(bf16[1024,1536]{1,0:T(8,128)(2,1)} %fusion.21), channel_id=1, source_target_pairs={{1,0},{2,1},{3,2},{5,4},{6,5},{7,6},{9,8},{10,9},{11,10},{13,12},{... | collective-permute-start | bytes 9437192 | tf_op jit(solution)/shard_map/ppermute | solution.py:17
  741.2 12.3 %collective-permute-start.3 = (f32[2,2304]{1,0:T(2,128)S(1)}, f32[2,2304]{1,0:T(2,128)S(1)}, u32[]{:S(2)}, u32[]{:S(2)}) collective-permute-start(f32[2,2304]{1,0:T(2,128)S(1)} %pad_maximum_fusion.8), channel_id=1, source_target_pairs={{1,0},{2,1},{3,2},{5,4},{6,5},{7,6},{9,8},{10,9},{11,10},{13,12},{... | collective-permute-start | bytes 55304 | tf_op jit(solution)/shard_map/ppermute | solution.py:17
  753.5 13.8 %copy-start.9 = (bf16[1024,768]{0,1:T(8,128)(2,1)S(1)}, bf16[1024,768]{0,1:T(8,128)(2,1)}, u32[]{:S(2)}) copy-start(bf16[1024,768]{0,1:T(8,128)(2,1)} %copy-done.7) | copy-start | bytes 4718596
  753.5 13.8 %copy-start.40 = (f32[768]{0:T(1024)S(1)}, f32[768]{0:T(1024)}, u32[]{:S(2)}) copy-start(f32[768]{0:T(1024)} %copy-done.39) | copy-start | bytes 9220
  753.5 13.8 %copy-start.42 = (f32[1024]{0:T(1024)S(1)}, f32[1024]{0:T(1024)}, u32[]{:S(2)}) copy-start(f32[1024]{0:T(1024)} %copy-done.41) | copy-start | bytes 12292
  823.2 312.2 %copy-start.10 = (bf16[1024,768]{0,1:T(8,128)(2,1)S(1)}, bf16[1024,768]{0,1:T(8,128)(2,1)}, u32[]{:S(2)}) copy-start(bf16[1024,768]{0,1:T(8,128)(2,1)} %copy-done.7) | copy-start | bytes 4718596
  1131.0 13.3 %collective-permute-start.4 = (f32[403,128]{1,0:T(8,128)}, f32[403,128]{1,0:T(8,128)}, u32[]{:S(2)}, u32[]{:S(2)}) collective-permute-start(f32[403,128]{1,0:T(8,128)} %slice.268), channel_id=1, source_target_pairs={{0,1},{1,2},{2,3},{3,4},{4,5},{5,6},{6,7},{7,8},{8,9},{9,10},{10,1... | collective-permute-start | bytes 619016
  (50 other events, 331.0 us)
Sparse Core Ops, SparseCore 0:
  11.5 106.0 all-gather.2
where the time goes:
time: 1170 us; the launch traced here: 1160 us
  matrix products  352 us (30%)
  blocking collectives  307 us (26%)
  other arithmetic  197 us (17%)
  local copies, waits for them, and re-layouts  166 us (14%)
  waiting for transfers between devices  105 us (9%)
  between operations  16.1 us (1%)
  starting transfers between devices  14.5 us (1%)
    unnamed x1, blocking collectives  307 us
    all_gather x1, waiting for transfers between devices, shards(): gathered = lax.all_gather(shard_low, ('dp', 'ctx'), axis=0, tiled=True)  95.1 us
    convert_element_type x2, other arithmetic, shards(): grad_scores = (probs_full * (grad_probs - inner_sum)).astype(jnp.bfloat16)  81 us
    dot_general x2, matrix products, shards(): jnp.einsum('qhd,khd->hqk', grad_heads[rows_part], value_heads, preferred_...  74.3 us
    unnamed x155, local copies, waits for them, and re-layouts  66.3 us
    dot_general x2, matrix products, shards(): jnp.einsum('hqk,qhd->khd', probs_low, grad_heads[rows_part], preferred_el...  48.3 us
    reduce_sum x2, other arithmetic, shards(): total_sum = jnp.sum(raised, axis=-1, keepdims=True)  45.8 us
    dot_general x2, matrix products, shards(): jnp.einsum('hqk,khd->qhd', probs_low, value_heads, preferred_element_type...  43.9 us
  transfers between devices with their start and end apart: 6, of which 3 were waited for; matrix products, arithmetic and copies ran while one was open for 8% of the time, Pallas kernels for 0%

commit v1 on v0

--- a/solution.py
+++ b/solution.py
@@ -1,3 +1,4 @@
+import functools
 import jax
 import jax.numpy as jnp
 from jax import lax
@@ -9,6 +10,32 @@
 FF = 3072
 SEQ_MIN = 1024
 norm_eps = 1e-06
+
+
+def use_turns_in(vector, axis_id):
+    taken_in, prior, g_now = (
+        jax.lax.psum(1, axis_id),
+        jax.lax.axis_index(axis_id),
+        vector.shape[0],
+    )
+    part_next, mid_arr = (vector, 1)
+    while mid_arr < taken_in:
+        part_next = jnp.concatenate(
+            [
+                part_next,
+                jax.lax.ppermute(
+                    part_next,
+                    axis_id,
+                    list(map(lambda no: (no, (no - mid_arr) % taken_in), range(taken_in))),
+                ),
+            ],
+            axis=0,
+        )
+        mid_arr = 2 * mid_arr
+    return jnp.roll(part_next, prior * g_now, axis=0)
+
+
+measure_thing_up = functools.partial(use_turns_in, axis_id=("dp", "ctx"))
 
 
 def from_behind(block, axis, distance):
@@ -95,7 +122,7 @@
     ctx_place = lax.axis_index("ctx")
     triple_width = 3 * D
     shard_low = master.astype(jnp.bfloat16)
-    gathered = lax.all_gather(shard_low, ("dp", "ctx"), axis=0, tiled=True)
+    gathered = measure_thing_up(shard_low)
     in_weight, out_weight, up_weight, down_weight, gain_first, gain_second, conv_taps = unpack(
         gathered
     )

time: 1170 us -> 1760 us (1.50)
  waiting for transfers between devices: 105 us -> 445 us
  local copies, waits for them, and re-layouts: 166 us -> 396 us
    ppermute x0 -> x5, waiting for transfers between devices: none -> 445 us  [use_turns_in(): jax.lax.ppermute(part_next, axis_id, list(map(lambda no: (no, (no - mid_a...]
    concatenate x1 -> x4, local copies, waits for them, and re-layouts: 1.35 us -> 175 us  [the longest x1 120 us: use_turns_in(): return jnp.roll(part_next, prior * g_now, axis=0)]
    all_gather x1, waiting for transfers between devices: 95.1 us -> 0.02 us  [shards(): regathered = lax.all_gather(shard_low, ('dp', 'ctx'), axis=0, tiled=True)]
    unnamed x155 -> x179, local copies, waits for them, and re-layouts: 66.3 us -> 72.7 us
  transfers between devices with their start and end apart: 6 -> 11, of which waited for: 3 -> 6; matrix products, arithmetic and copies ran while one was open for 8% -> 27% of each run, Pallas kernels for 0% -> 0%
where the time goes in v1:
time: 1760 us; the launch traced here: 1740 us
  waiting for transfers between devices  445 us (25%)
  local copies, waits for them, and re-layouts  396 us (22%)
  matrix products  353 us (20%)
  blocking collectives  302 us (17%)
  other arithmetic  203 us (12%)
  starting transfers between devices  27.8 us (2%)
    ppermute x5, waiting for transfers between devices, use_turns_in(): jax.lax.ppermute(part_next, axis_id, list(map(lambda no: (no, (no - mid_a...  445 us
    unnamed x1, blocking collectives  302 us
    concatenate x1, local copies, waits for them, and re-layouts, use_turns_in(): return jnp.roll(part_next, prior * g_now, axis=0)  120 us
    convert_element_type x2, other arithmetic, shards(): grad_scores = (probs_full * (grad_probs - inner_sum)).astype(jnp.bfloat16)  82.2 us
    dot_general x2, matrix products, shards(): jnp.einsum('qhd,khd->hqk', grad_heads[rows_part], value_heads, preferred_...  75.5 us
    unnamed x179, local copies, waits for them, and re-layouts  72.7 us
    concatenate x3, local copies, waits for them, and re-layouts, use_turns_in(): jnp.concatenate([part_next, jax.lax.ppermute(part_next, axis_id, list(map...  54.8 us
    dot_general x2, matrix products, shards(): jnp.einsum('hqk,qhd->khd', probs_low, grad_heads[rows_part], preferred_el...  48.3 us
  transfers between devices with their start and end apart: 11, of which 6 were waited for; matrix products, arithmetic and copies ran while one was open for 27% of the time, Pallas kernels for 0%

profile of v1, /device:TPU:1, one launch (start us, length us, event | category | flops | bytes accessed | tf_op | source)
XLA Modules:
  0.0 1742.9 jit_solution(2095938853412040580)
XLA Ops:
  26.1 15.2 collective-permute-done.1
  51.9 38.1 %collective-permute-done.2 = bf16[6924,128]{1,0:T(8,128)(2,1)S(1)} collective-permute-done((bf16[6924,128]{1,0:T(8,128)(2,1)}, bf16[6924,128]{1,0:T(8,128)(2,1)S(1)}, u32[]{:S(2)}, u32[]{:S(2)}) %collective-permute-start.2) | collective-permute-done | bytes 1772576 | tf_op jit(solution)/shard_map/ppermute | solution.py:26
  91.2 16.1 concatenate.62
  108.6 77.1 %collective-permute-done.3 = bf16[13848,128]{1,0:T(8,128)(2,1)S(1)} collective-permute-done((bf16[13848,128]{1,0:T(8,128)(2,1)}, bf16[13848,128]{1,0:T(8,128)(2,1)S(1)}, u32[]{:S(2)}, u32[]{:S(2)}) %collective-permute-start.3) | collective-permute-done | bytes 3545120 | tf_op jit(solution)/shard_map/ppermute | solution.py:26
  185.8 29.9 %concatenate.63 = bf16[27696,128]{1,0:T(8,128)(2,1)} concatenate(bf16[1731,128]{1,0:T(8,128)(2,1)} %copy-done.12, bf16[1731,128]{1,0:T(8,128)(2,1)} %copy-done.14, bf16[3462,128]{1,0:T(8,128)(2,1)} %copy-done.11, bf16[6924,128]{1,0:T(8,128)(2,1)} %copy-done.9, bf16[13848,128]{1,0:T(8,128)(2,1)S(1)} %collective-permute-done.3), dimensions={0} | concatenate | bytes 14180352 | tf_op jit(solution)/shard_map/concatenate | solution.py:23
  226.4 305.7 %collective-permute-done.4 = bf16[27696,128]{1,0:T(8,128)(2,1)} collective-permute-done((bf16[27696,128]{1,0:T(8,128)(2,1)}, bf16[27696,128]{1,0:T(8,128)(2,1)}, u32[]{:S(2)}, u32[]{:S(2)}) %collective-permute-start.4) | collective-permute-done | bytes 7090208 | tf_op jit(solution)/shard_map/ppermute | solution.py:26
  532.0 119.8 %concatenate.64 = bf16[110784,128]{1,0:T(8,128)(2,1)} concatenate(bf16[1731,128]{1,0:T(8,128)(2,1)} %copy-done.12, bf16[1731,128]{1,0:T(8,128)(2,1)} %copy-done.14, bf16[3462,128]{1,0:T(8,128)(2,1)} %copy-done.11, bf16[6924,128]{1,0:T(8,128)(2,1)} %copy-done.9, bf16[13848,128]{1,0:T(8,128)(2,1)S(1)} %collective-permute-done.3, bf16[27696,128]{1,0:T(8,128)(2,1)} %collective-permute-done.4, ...), dimensions={0} | concatenate | bytes 56721408 | tf_op jit(solution)/shard_map/jit(_roll_dynamic)/concatenate | solution.py:35
  749.9 21.5 %fusion.13 = (f32[12,512]{1,0:T(8,128)S(1)}, f32[12,512,2048]{2,1,0:T(8,128)}) fusion(pred[512,2048]{1,0:T(8,128)(4,1)} %get-tuple-element.72, bf16[512,12,64]{0,2,1:T(8,128)(2,1)} %bitcast.136, bf16[2048,12,64]{0,2,1:T(8,128)(2,1)S(1)} %bitcast.117), kind=kOutput, calls=%fused_computation.27 | convolution fusion | flops 1648355328 | bytes 55336960 | tf_op jit(solution)/shard_map/qhd,khd->hqk/dot_general | solution.py:87
  771.4 22.2 %fusion.1 = f32[12,512]{1,0:T(8,128)S(1)} fusion(f32[12,512]{1,0:T(8,128)S(1)} %get-tuple-element.85, f32[12,512,2048]{2,1,0:T(8,128)} %get-tuple-element.86, pred[512,2048]{1,0:T(8,128)(4,1)} %get-tuple-element.72), kind=kLoop, calls=%fused_computation.12 | loop fusion | flops 50325504 | bytes 51429376 | tf_op jit(solution)/shard_map/reduce_sum | solution.py:165
  793.6 21.5 %fusion.14 = (f32[12,512]{1,0:T(8,128)S(1)}, f32[12,512,2048]{2,1,0:T(8,128)}) fusion(pred[512,2048]{1,0:T(8,128)(4,1)} %get-tuple-element.73, bf16[512,12,64]{0,2,1:T(8,128)(2,1)} %bitcast.134, bf16[2048,12,64]{0,2,1:T(8,128)(2,1)S(1)} %bitcast.118), kind=kOutput, calls=%fused_computation.28 | convolution fusion | flops 1648355328 | bytes 55336960 | tf_op jit(solution)/shard_map/qhd,khd->hqk/dot_general | solution.py:87
  815.1 22.5 %fusion.2 = f32[12,512]{1,0:T(8,128)S(1)} fusion(f32[12,512]{1,0:T(8,128)S(1)} %get-tuple-element.83, f32[12,512,2048]{2,1,0:T(8,128)} %get-tuple-element.84, pred[512,2048]{1,0:T(8,128)(4,1)} %get-tuple-element.73), kind=kLoop, calls=%fused_computation.13 | loop fusion | flops 50325504 | bytes 51429376 | tf_op jit(solution)/shard_map/reduce_sum | solution.py:165
  837.7 21.0 %fusion.51 = bf16[12,64,512]{2,1,0:T(8,128)(2,1)} fusion(bf16[2048,12,64]{0,2,1:T(8,128)(2,1)S(1)} %bitcast.128, f32[12,512]{1,0:T(8,128)S(1)} %fusion.1, f32[12,512]{1,0:T(8,128)S(1)} %get-tuple-element.85, f32[12,512,2048]{2,1,0:T(8,128)} %get-tuple-element.86, pred[512,2048]{1,0:T(8,128)(4,1)S(1)} %copy-done.6), kind=kOutput, calls=%fused_computation.101 | convolution fusion | flops 1673920512 | bytes 55361536 | tf_op jit(solution)/shard_map/hqk,khd->qhd/dot_general | solution.py:167
  858.7 21.3 %fusion.50 = bf16[12,64,512]{2,1,0:T(8,128)(2,1)} fusion(bf16[2048,12,64]{0,2,1:T(8,128)(2,1)S(1)} %bitcast.129, f32[12,512]{1,0:T(8,128)S(1)} %fusion.2, f32[12,512]{1,0:T(8,128)S(1)} %get-tuple-element.83, f32[12,512,2048]{2,1,0:T(8,128)} %get-tuple-element.84, pred[512,2048]{1,0:T(8,128)(4,1)S(1)} %copy-done.4), kind=kOutput, calls=%fused_computation.100 | convolution fusion | flops 1673920512 | bytes 55361536 | tf_op jit(solution)/shard_map/hqk,khd->qhd/dot_general | solution.py:167
  996.7 37.4 %multiply_reduce_fusion.1 = (f32[12,512]{1,0:T(8,128)S(1)}, f32[12,512,2048]{2,1,0:T(8,128)}) fusion(f32[12,512]{1,0:T(8,128)S(1)} %log_add_fusion.1, f32[12,512,2048]{2,1,0:T(8,128)} %get-tuple-element.86, pred[512,2048]{1,0:T(8,128)(4,1)S(1)} %copy-done.7, bf16[512,12,64]{0,2,1:T(8,128)(2,1)S(1)} %bitcast.139, bf16[2048,12,64]{0,2,1:T(8,128)(2,1)} %bitcast.126), kind=kOutput, calls=%fused_computation.4 | convolution fusion | flops 1673521152 | bytes 105693184 | tf_op jit(solution)/shard_map/qhd,khd->hqk/dot_general | solution.py:219
  1034.1 41.8 %multiply_convert_fusion.1 = bf16[12,512,2048]{2,1,0:T(8,128)(2,1)} fusion(f32[12,512,2048]{2,1,0:T(8,128)} %get-tuple-element.91, f32[12,512]{1,0:T(8,128)S(1)} %get-tuple-element.90, f32[12,512]{1,0:T(8,128)S(1)} %log_add_fusion.1, f32[12,512,2048]{2,1,0:T(8,128)} %get-tuple-element.86, pred[512,2048]{1,0:T(8,128)(4,1)} %get-tuple-element.72), kind=kLoop, calls=%fused_computation.3 | loop fusion | flops 75497472 | bytes 126926848 | tf_op jit(solution)/shard_map/convert_element_type | solution.py:223
  1089.6 15.7 fusion.102
  1105.3 23.0 %fusion.5 = f32[12,64,2048]{2,1,0:T(8,128)} fusion(bf16[512,12,64]{0,2,1:T(8,128)(2,1)S(1)} %bitcast.142, f32[12,512]{1,0:T(8,128)S(1)} %log_add_fusion, f32[12,512,2048]{2,1,0:T(8,128)} %get-tuple-element.84, pred[512,2048]{1,0:T(8,128)(4,1)S(1)} %copy-done.5), kind=kOutput, calls=%fused_computation.16 | convolution fusion | flops 1660944384 | bytes 58482688 | tf_op jit(solution)/shard_map/hqk,qhd->khd/dot_general | solution.py:238
  1128.2 38.1 %multiply_reduce_fusion = (f32[12,512]{1,0:T(8,128)S(1)}, f32[12,512,2048]{2,1,0:T(8,128)}) fusion(f32[12,512]{1,0:T(8,128)S(1)} %log_add_fusion, f32[12,512,2048]{2,1,0:T(8,128)} %get-tuple-element.84, pred[512,2048]{1,0:T(8,128)(4,1)S(1)} %copy-done.5, bf16[512,12,64]{0,2,1:T(8,128)(2,1)} %bitcast.141, bf16[2048,12,64]{0,2,1:T(8,128)(2,1)} %bitcast.127), kind=kOutput, calls=%fused_computation.1 | convolution fusion | flops 1673521152 | bytes 105693184 | tf_op jit(solution)/shard_map/qhd,khd->hqk/dot_general | solution.py:219
  1166.3 25.4 %fusion.37 = f32[12,64,2048]{2,1,0:T(8,128)} fusion(f32[12,64,2048]{2,1,0:T(8,128)} %fusion.5, bf16[512,12,64]{0,2,1:T(8,128)(2,1)S(1)} %bitcast.140, f32[12,512]{1,0:T(8,128)S(1)} %log_add_fusion.1, f32[12,512,2048]{2,1,0:T(8,128)} %get-tuple-element.86, pred[512,2048]{1,0:T(8,128)(4,1)S(1)} %copy-done.8), kind=kOutput, calls=%fused_computation.76 | convolution fusion | flops 1662517248 | bytes 64774144 | tf_op jit(solution)/shard_map/hqk,qhd->khd/dot_general | solution.py:238
  1198.2 40.4 %multiply_convert_fusion = bf16[12,512,2048]{2,1,0:T(8,128)(2,1)} fusion(f32[12,512,2048]{2,1,0:T(8,128)} %get-tuple-element.93, f32[12,512]{1,0:T(8,128)S(1)} %get-tuple-element.92, f32[12,512]{1,0:T(8,128)S(1)} %log_add_fusion, f32[12,512,2048]{2,1,0:T(8,128)} %get-tuple-element.84, pred[512,2048]{1,0:T(8,128)(4,1)S(1)} %copy-done.5), kind=kLoop, calls=%fused_computation | loop fusion | flops 75497472 | bytes 126926848 | tf_op jit(solution)/shard_map/convert_element_type | solution.py:223
  1238.6 17.1 add_multiply_fusion
  1301.6 13.8 multiply_bitcast_fusion
  1342.5 13.7 multiply_reduce_fusion.4
  1411.1 302.4 %fusion = f32[1744,128]{1,0:T(8,128)S(1)} fusion(f32[55392,128]{1,0:T(8,128)} %bitcast.31), kind=kCustom, calls=%all-reduce-scatter | all-reduce-scatter fusion | flops 7143425 | bytes 29253632
  (296 shorter events, 426.3 us)
Async XLA Ops:
  7.2 919.4 %all-gather.3.cloned.1.call-start = ((), (), s32[]{:S(2)}) async-start(), calls=%async_computation | async-start | bytes 14665728 | tf_op jit(solution)/shard_map/all_gather | solution.py:182
  8.4 81.5 %copy-start.12 = (bf16[1731,128]{1,0:T(8,128)(2,1)}, bf16[1731,128]{1,0:T(8,128)(2,1)S(1)}, u32[]{:S(2)}) copy-start(bf16[1731,128]{1,0:T(8,128)(2,1)S(1)} %convert_element_type.133) | copy-start | bytes 1329412
  8.4 8.7 collective-permute-start
  17.1 72.8 %copy-start.14 = (bf16[1731,128]{1,0:T(8,128)(2,1)}, bf16[1731,128]{1,0:T(8,128)(2,1)S(1)}, u32[]{:S(2)}) copy-start(bf16[1731,128]{1,0:T(8,128)(2,1)S(1)} %collective-permute-done) | copy-start | bytes 1329412
  17.3 24.0 %collective-permute-start.1 = (bf16[3462,128]{1,0:T(8,128)(2,1)S(1)}, bf16[3462,128]{1,0:T(8,128)(2,1)S(1)}, u32[]{:S(2)}, u32[]{:S(2)}) collective-permute-start(bf16[3462,128]{1,0:T(8,128)(2,1)S(1)} %pad_maximum_fusion.7), channel_id=1, source_target_pairs={{0,30},{1,31},{2,0},{3,1},{4,2},{5,3},{6,4},{7,5},{8,6},{9,7},{10,... | collective-permute-start | bytes 2658824 | tf_op jit(solution)/shard_map/ppermute | solution.py:26
  41.2 48.7 %copy-start.11 = (bf16[3462,128]{1,0:T(8,128)(2,1)}, bf16[3462,128]{1,0:T(8,128)(2,1)S(1)}, u32[]{:S(2)}) copy-start(bf16[3462,128]{1,0:T(8,128)(2,1)S(1)} %collective-permute-done.1) | copy-start | bytes 2658820
  50.0 39.9 %collective-permute-start.2 = (bf16[6924,128]{1,0:T(8,128)(2,1)}, bf16[6924,128]{1,0:T(8,128)(2,1)S(1)}, u32[]{:S(2)}, u32[]{:S(2)}) collective-permute-start(bf16[6924,128]{1,0:T(8,128)(2,1)} %concatenate.61), channel_id=1, source_target_pairs={{0,28},{1,29},{2,30},{3,31},{4,0},{5,1},{6,2},{7,3},{8,4},{9,5},{1... | collective-permute-start | bytes 5317640 | tf_op jit(solution)/shard_map/ppermute | solution.py:26
  107.3 78.5 %collective-permute-start.3 = (bf16[13848,128]{1,0:T(8,128)(2,1)}, bf16[13848,128]{1,0:T(8,128)(2,1)S(1)}, u32[]{:S(2)}, u32[]{:S(2)}) collective-permute-start(bf16[13848,128]{1,0:T(8,128)(2,1)} %concatenate.62), channel_id=1, source_target_pairs={{0,24},{1,25},{2,26},{3,27},{4,28},{5,29},{6,30},{7,31},{8,0},{9,1... | collective-permute-start | bytes 10635272 | tf_op jit(solution)/shard_map/ppermute | solution.py:26
  215.7 316.3 %collective-permute-start.4 = (bf16[27696,128]{1,0:T(8,128)(2,1)}, bf16[27696,128]{1,0:T(8,128)(2,1)}, u32[]{:S(2)}, u32[]{:S(2)}) collective-permute-start(bf16[27696,128]{1,0:T(8,128)(2,1)} %concatenate.63), channel_id=1, source_target_pairs={{0,16},{1,17},{2,18},{3,19},{4,20},{5,21},{6,22},{7,23},{8,24},{9,... | collective-permute-start | bytes 21270536 | tf_op jit(solution)/shard_map/ppermute | solution.py:26
  226.4 463.8 %copy-start.46 = (f32[1024]{0:T(1024)}, f32[1024]{0:T(1024)S(1)}, u32[]{:S(2)}) copy-start(f32[1024]{0:T(1024)S(1)} %get-tuple-element.77) | copy-start | bytes 12292
  226.4 464.5 %copy-start.48 = (f32[1024]{0:T(1024)}, f32[1024]{0:T(1024)S(1)}, u32[]{:S(2)}) copy-start(f32[1024]{0:T(1024)S(1)} %get-tuple-element.78) | copy-start | bytes 12292
  673.6 3.4 collective-permute-start.5
  684.8 50.3 %collective-permute-start.6 = (bf16[1024,1536]{1,0:T(8,128)(2,1)S(1)}, bf16[1024,1536]{1,0:T(8,128)(2,1)}, u32[]{:S(2)}, u32[]{:S(2)}) collective-permute-start(bf16[1024,1536]{1,0:T(8,128)(2,1)S(1)} %slice.287), channel_id=1, source_target_pairs={{0,1},{1,2},{2,3},{4,5},{5,6},{6,7},{8,9},{9,10},{10,11},{12,13},{... | collective-permute-start | bytes 9437192 | tf_op jit(solution)/shard_map/ppermute | solution.py:44
  744.4 49.2 %copy-start.1 = (bf16[2048,768]{0,1:T(8,128)(2,1)}, bf16[2048,768]{0,1:T(8,128)(2,1)S(1)}, u32[]{:S(2)}) copy-start(bf16[2048,768]{0,1:T(8,128)(2,1)S(1)} %copy.56) | copy-start | bytes 9437188
  883.2 109.7 %copy-start.20 = (f32[1024,768]{0,1:T(8,128)}, f32[1024,768]{0,1:T(8,128)S(1)}, u32[]{:S(2)}) copy-start(f32[1024,768]{0,1:T(8,128)S(1)} %get-tuple-element.88) | copy-start | bytes 9437188
  883.3 109.7 %copy-start.42 = (f32[1024]{0:T(1024)}, f32[1024]{0:T(1024)S(1)}, u32[]{:S(2)}) copy-start(f32[1024]{0:T(1024)S(1)} %add_rsqrt_fusion) | copy-start | bytes 12292
  1034.1 41.8 %copy-start.2 = (bf16[2048,768]{0,1:T(8,128)(2,1)S(1)}, bf16[2048,768]{0,1:T(8,128)(2,1)}, u32[]{:S(2)}) copy-start(bf16[2048,768]{0,1:T(8,128)(2,1)} %copy-done.1) | copy-start | bytes 9437188
  1128.2 38.1 %copy-start.8 = (pred[512,2048]{1,0:T(8,128)(4,1)S(1)}, pred[512,2048]{1,0:T(8,128)(4,1)}, u32[]{:S(2)}) copy-start(pred[512,2048]{1,0:T(8,128)(4,1)} %get-tuple-element.72) | copy-start | bytes 3145732
  1128.2 38.1 %copy-start.34 = (bf16[512,768]{0,1:T(8,128)(2,1)S(1)}, bf16[512,768]{0,1:T(8,128)(2,1)}, u32[]{:S(2)}) copy-start(bf16[512,768]{0,1:T(8,128)(2,1)} %copy-done.33) | copy-start | bytes 2359300
  1198.2 40.4 %copy-start.26 = (bf16[512,768]{0,1:T(8,128)(2,1)S(1)}, bf16[512,768]{0,1:T(8,128)(2,1)}, u32[]{:S(2)}) copy-start(bf16[512,768]{0,1:T(8,128)(2,1)} %copy.57) | copy-start | bytes 2359300
  1267.3 57.0 %collective-permute-start.7 = (bf16[1024,1536]{1,0:T(8,128)(2,1)}, bf16[1024,1536]{1,0:T(8,128)(2,1)}, u32[]{:S(2)}, u32[]{:S(2)}) collective-permute-start(bf16[1024,1536]{1,0:T(8,128)(2,1)} %fusion.21), channel_id=1, source_target_pairs={{1,0},{2,1},{3,2},{5,4},{6,5},{7,6},{9,8},{10,9},{11,10},{13,12},{... | collective-permute-start | bytes 9437192 | tf_op jit(solution)/shard_map/ppermute | solution.py:44
  1328.7 12.4 collective-permute-start.8
  1411.1 307.5 %copy-start.18 = (bf16[1024,768]{0,1:T(8,128)(2,1)S(1)}, bf16[1024,768]{0,1:T(8,128)(2,1)}, u32[]{:S(2)}) copy-start(bf16[1024,768]{0,1:T(8,128)(2,1)} %copy.53) | copy-start | bytes 4718596
  1714.2 13.3 collective-permute-start.9
  (68 other events, 666.1 us)
Sparse Core Ops, SparseCore 0:
  217.8 393.6 all-gather.2
